TPU v7x, 32 devices: a whole 2x2x4 slice. The times are simulated.
32 devices in a mesh: expert: 8 (over z, x), tensor: 4 (over y, core).
Axes of the slice: x: 2, y: 2, z: 4, core: 2. Of those that a mesh axis runs over, the one named last changes fastest.
Arguments:
- tokens: bfloat16 [1024, 4096], P('expert', 'tensor'), may hold values from -6 to 6
- expert_ids: int32 [1024, 8], P('expert'), may hold values from 0 to 15, all different within a row; in each aligned block of 128 rows (0 to 127, 128 to 255, ...) at most 96 rows name the same one
- combine_weight: float32 [1024, 8], P('expert'), may hold values from 0.05 to 0.5
- gate_weight: bfloat16 [16, 4096, 1024], P('expert', 'tensor'), may hold values from -0.09375 to 0.09375
- up_weight: bfloat16 [16, 4096, 1024], P('expert', 'tensor'), may hold values from -0.09375 to 0.09375
- down_weight: bfloat16 [16, 1024, 4096], P('expert', None, 'tensor'), may hold values from -0.1875 to 0.1875
- out_cotangent: bfloat16 [1024, 4096], P('expert', 'tensor'), may hold values from -3 to 3
Outputs:
- mixed: bfloat16 [1024, 4096], P('expert', 'tensor')
- token_grad: bfloat16 [1024, 4096], P('expert', 'tensor')
- combine_grad: float32 [1024, 8], P('expert')
- gate_grad: bfloat16 [16, 4096, 1024], P('expert', 'tensor')
- up_grad: bfloat16 [16, 4096, 1024], P('expert', 'tensor')
- down_grad: bfloat16 [16, 1024, 4096], P('expert', None, 'tensor')
Inputs may be any that keep to these rules, and one draw needn't show every extreme that they name: `expert_ids`: each row names 8 different experts. Among the rows of one device no expert is named by more than 96 rows, a bound that some block reaches.
All inputs are finite; a program needn't handle non-finite values.
Results may differ from a plain program's by a relative error of at most 0.023.
Values may be sent and summed in bfloat16 or wider, within the bound.
A program may use at most 128 MiB of HBM per device.

v0:
```python
import jax
import jax.numpy as jnp
from jax import lax
from jax.sharding import PartitionSpec as P

F32, BF16 = (jnp.float32, jnp.bfloat16)


def dot(form, left, right):
    return jnp.einsum(form, left, right, preferred_element_type=F32)


def per_device(
    tokens, expert_ids, combine_weight, gate_weight, up_weight, down_weight, out_cotangent
):
    groups = lax.axis_size("expert")
    shards = lax.axis_size("tensor")
    local = gate_weight.shape[0]
    width = tokens.shape[1]
    hidden = gate_weight.shape[2]
    rows = tokens.shape[0]
    top = expert_ids.shape[1]
    experts = local * groups
    capacity = 3 * rows * top // (2 * experts)
    slots = groups * capacity
    total = local * slots
    own = total // shards
    mine = lax.axis_index("expert")
    named = expert_ids[:, :, None] == jnp.arange(experts, dtype=jnp.int32)
    dense_weight = jnp.sum(jnp.where(named, combine_weight[:, :, None], 0.0), axis=1)
    weights_all = lax.all_gather(dense_weight, "expert", axis=0)
    tokens_all = lax.all_gather(tokens, "expert", axis=0)
    cotangent_all = lax.all_gather(out_cotangent, "expert", axis=0)
    weight_tok = lax.dynamic_slice_in_dim(weights_all, mine * local, local, 2)
    weight_tok = weight_tok.transpose(2, 0, 1)
    served = weight_tok > 0.0
    earlier = (jnp.arange(rows)[:, None] < jnp.arange(rows)[None, :]).astype(BF16)
    position = dot("ebs,st->ebt", served.astype(BF16), earlier)
    at_slot = jnp.where(served, position, -1.0).astype(jnp.int32)
    chosen = at_slot[:, :, None, :] == jnp.arange(capacity, dtype=jnp.int32)[:, None]
    place = chosen.astype(BF16)
    weight_slot = jnp.sum(jnp.where(chosen, weight_tok[:, :, None, :], 0.0), axis=3)
    weight_slot = weight_slot.reshape(total, 1)
    weight_own = lax.dynamic_slice_in_dim(weight_slot, lax.axis_index("tensor") * own, own, 0)

    def dispatch(values):
        return [
            dot("bct,btd->bcd", place[e], values).astype(BF16).reshape(slots, width)
            for e in range(local)
        ]

    def scatter_rows(parts):
        return lax.psum_scatter(
            jnp.concatenate(parts, axis=0), "tensor", scatter_dimension=0, tiled=True
        ).astype(F32)

    def gather_rows(value):
        full = lax.all_gather(value.astype(BF16), "tensor", axis=0, tiled=True)
        return full.reshape(local, slots, hidden)

    def combine(parts):
        total_sum = sum(
            (
                dot("bct,bcd->btd", place[e], parts[e].reshape(groups, capacity, width))
                for e in range(local)
            )
        )
        return lax.psum_scatter(
            total_sum.astype(BF16), "expert", scatter_dimension=0, tiled=True
        ).reshape(rows, width)

    routed = dispatch(tokens_all)
    gate = scatter_rows(
        [dot("cd,dk->ck", routed[e], gate_weight[e]).astype(BF16) for e in range(local)]
    )
    up = scatter_rows(
        [dot("cd,dk->ck", routed[e], up_weight[e]).astype(BF16) for e in range(local)]
    )
    incoming = dispatch(cotangent_all)
    pulled = scatter_rows(
        [dot("cd,kd->ck", incoming[e], down_weight[e]).astype(BF16) for e in range(local)]
    )
    sigma = jax.nn.sigmoid(gate)
    silu = gate * sigma
    act = silu * up
    weighted_act = gather_rows(weight_own * act)
    weighted_pull = weight_own * pulled
    gate_diff = gather_rows(weighted_pull * up * sigma * (1.0 + gate * (1.0 - sigma)))
    up_diff = gather_rows(weighted_pull * silu)
    pair_own = jnp.sum(act * pulled, axis=1)
    pair_all = lax.all_gather(pair_own, "tensor", axis=0, tiled=True)
    pair_all = pair_all.reshape(local, groups, capacity)
    pair_tok = jnp.sum(jnp.where(chosen, pair_all[:, :, :, None], 0.0), axis=2)
    pair_tok = lax.all_to_all(
        pair_tok.transpose(1, 0, 2), "expert", split_axis=0, concat_axis=0, tiled=True
    ).reshape(experts, rows)
    combine_grad = jnp.sum(jnp.where(named, pair_tok.T[:, None, :], 0.0), axis=2)
    mixed = combine(
        [dot("ck,kd->cd", weighted_act[e], down_weight[e]).astype(BF16) for e in range(local)]
    )
    token_grad = combine(
        [
            (
                dot("ck,dk->cd", gate_diff[e], gate_weight[e])
                + dot("ck,dk->cd", up_diff[e], up_weight[e])
            ).astype(BF16)
            for e in range(local)
        ]
    )
    down_grad = jnp.stack(
        [dot("ck,cd->kd", weighted_act[e], incoming[e]).astype(BF16) for e in range(local)]
    )
    gate_grad = jnp.stack(
        [dot("cd,ck->dk", routed[e], gate_diff[e]).astype(BF16) for e in range(local)]
    )
    up_grad = jnp.stack(
        [dot("cd,ck->dk", routed[e], up_diff[e]).astype(BF16) for e in range(local)]
    )
    return (mixed, token_grad, combine_grad, gate_grad, up_grad, down_grad)


def solution(mesh):
    wide, narrow = (P("expert", "tensor"), P("expert", None))
    deep, flat = (P("expert", "tensor", None), P("expert", None, "tensor"))
    return jax.shard_map(
        per_device,
        mesh=mesh,
        in_specs=(wide, narrow, narrow, deep, deep, flat, wide),
        out_specs=(wide, wide, narrow, deep, deep, flat),
        check_vma=False,
    )
```

profile of v0, /device:TPU:0, one launch (start us, length us, event | category | flops | bytes accessed | tf_op | source)
XLA Modules:
  0.0 485.3 jit_solution(2494550937460764869)
XLA Ops:
  7.2 0.7 all-gather.16.cloned.1.call-update
  7.9 0.7 all-gather.18.cloned.1.call-update
  8.7 0.7 select_reduce_fusion.3
  9.4 32.6 %all-gather = f32[1024,16]{0,1:T(8,128)S(1)} all-gather(f32[128,16]{0,1:T(8,128)S(1)} %select_reduce_fusion.3), channel_id=2, replica_groups=mesh['expert'=8,'tensor'=4] {'expert'}, dimensions={0}, use_global_device_ids=true | all-gather | bytes 73728 | tf_op jit(solution)/shard_map/all_gather | solution.py:31
  42.3 20.0 %all-gather.16.cloned.1.call-done = bf16[1024,1024]{1,0:T(8,128)(2,1)} async-done(((bf16[128,1024]{1,0:T(8,128)(2,1)}), bf16[1024,1024]{1,0:T(8,128)(2,1)}) %all-gather.16.cloned.1.call-update) | async-done | bytes 2097168 | tf_op jit(solution)/shard_map/all_gather | solution.py:32
  62.3 2.3 convolution_convert_fusion.2
  64.6 0.6 convolution_convert_fusion.3
  65.2 0.8 copy-done.16
  66.0 1.8 fusion.46
  67.8 1.8 fusion.43
  69.6 2.0 pad_maximum_fusion.4
  71.7 40.4 %all-gather.18.cloned.1.call-done = bf16[1024,1024]{1,0:T(8,128)(2,1)} async-done(((bf16[128,1024]{1,0:T(8,128)(2,1)}), bf16[1024,1024]{1,0:T(8,128)(2,1)}) %all-gather.18.cloned.1.call-update) | async-done | bytes 2097168 | tf_op jit(solution)/shard_map/all_gather | solution.py:33
  112.1 2.3 convolution_convert_fusion
  114.4 0.6 convolution_convert_fusion.1
  115.0 0.8 copy-done.14
  115.8 1.8 fusion.58
  117.7 1.8 fusion.52
  119.5 2.0 pad_maximum_fusion.5
  121.5 0.5 reduce-scatter.6.cloned.1.call-start
  122.0 3.7 fusion.40
  125.7 1.8 fusion.37
  127.5 2.0 pad_maximum_fusion.3
  129.6 22.1 %reduce-scatter.8.cloned.1.call-done = bf16[384,1024]{1,0:T(8,128)(2,1)} async-done(((bf16[1536,1024]{1,0:T(8,128)(2,1)}), bf16[384,1024]{1,0:T(8,128)(2,1)}) %reduce-scatter.8.cloned.1.call-update) | async-done | bytes 786448 | tf_op jit(solution)/shard_map/reduce_scatter | solution.py:53
  151.6 40.9 %reduce-scatter.12.cloned.1.call-done = bf16[384,1024]{1,0:T(8,128)(2,1)} async-done(((bf16[1536,1024]{1,0:T(8,128)(2,1)}), bf16[384,1024]{1,0:T(8,128)(2,1)}) %reduce-scatter.12.cloned.1.call-update) | async-done | bytes 786448 | tf_op jit(solution)/shard_map/reduce_scatter | solution.py:53
  192.5 40.9 %reduce-scatter.6.cloned.1.call-done = bf16[384,1024]{1,0:T(8,128)(2,1)} async-done(((bf16[1536,1024]{1,0:T(8,128)(2,1)}), bf16[384,1024]{1,0:T(8,128)(2,1)}) %reduce-scatter.6.cloned.1.call-update) | async-done | bytes 786448 | tf_op jit(solution)/shard_map/reduce_scatter | solution.py:53
  233.4 2.3 fusion.65
  235.7 5.2 %all-gather.3 = f32[4,1,384]{2,1,0:T(1,128)S(1)} all-gather(f32[1,1,384]{2,1,0:T(1,128)S(1)} %reshape.84), channel_id=1, replica_groups=mesh['expert'=8,'tensor'=4] {'tensor'}, dimensions={0}, use_global_device_ids=true | all-gather | bytes 7680 | tf_op jit(solution)/shard_map/all_gather | solution.py:91
  241.0 0.6 select_reduce_fusion
  241.8 2.6 fusion.64
  244.4 0.7 all-gather.14.cloned.1.call-update
  245.1 0.7 all-gather.12.cloned.1.call-update
  245.9 27.1 %all-gather.10.cloned.1.call-done = bf16[1536,1024]{1,0:T(8,128)(2,1)} async-done(((bf16[384,1024]{1,0:T(8,128)(2,1)}), bf16[1536,1024]{1,0:T(8,128)(2,1)}) %all-gather.10.cloned.1.call-update) | async-done | bytes 3145744 | tf_op jit(solution)/shard_map/all_gather | solution.py:58
  273.0 4.0 fusion.49
  277.0 0.8 fusion.88
  277.8 1.4 copy-done.15
  279.2 1.8 fusion.55
  281.0 2.1 add_convert_fusion.1
  283.1 0.2 reduce-scatter.14.cloned.1.call-start
  283.3 20.3 %all-gather.14.cloned.1.call-done = bf16[1536,1024]{1,0:T(8,128)(2,1)} async-done(((bf16[384,1024]{1,0:T(8,128)(2,1)}), bf16[1536,1024]{1,0:T(8,128)(2,1)}) %all-gather.14.cloned.1.call-update) | async-done | bytes 3145744 | tf_op jit(solution)/shard_map/all_gather | solution.py:58
  303.7 3.9 fusion.12
  307.6 26.8 %all-gather.12.cloned.1.call-done = bf16[1536,1024]{1,0:T(8,128)(2,1)} async-done(((bf16[384,1024]{1,0:T(8,128)(2,1)}), bf16[1536,1024]{1,0:T(8,128)(2,1)}) %all-gather.12.cloned.1.call-update) | async-done | bytes 3145744 | tf_op jit(solution)/shard_map/all_gather | solution.py:58
  334.3 4.1 add_convert_fusion.3
  338.4 0.8 fusion.87
  339.2 1.4 copy-done.17
  340.6 1.8 fusion.8
  342.4 0.3 copy-done.19
  342.8 1.0 copy-done.24
  343.8 1.8 add_convert_fusion.2
  345.6 2.2 add_convert_fusion
  347.9 12.2 %all_to_all.5 = f32[8,2,128]{2,1,0:T(2,128)S(1)} all-to-all(f32[8,2,128]{2,1,0:T(2,128)S(1)} %copy.26), channel_id=1, replica_groups=mesh['expert'=8,'tensor'=4] {'expert'}, dimensions={0} | all-to-all | bytes 16384 | tf_op jit(solution)/shard_map/all_to_all | solution.py:94
  360.0 0.6 select_reduce_fusion.2
  360.7 3.4 convert_bitcast_fusion.4
  364.1 1.9 convert_bitcast_fusion.5
  366.0 2.5 pad_maximum_fusion
  368.5 0.9 copy-done.23
  369.4 1.9 convert_bitcast_fusion.2
  371.2 1.9 convert_bitcast_fusion.3
  373.1 2.5 pad_maximum_fusion.1
  375.6 1.4 copy-done.21
  377.0 1.9 convert_bitcast_fusion
  378.9 1.9 convert_bitcast_fusion.1
  380.7 2.4 pad_maximum_fusion.2
  383.1 23.7 %reduce-scatter.10.cloned.1.call-done = bf16[1,128,1024]{2,1,0:T(8,128)(2,1)} async-done(((bf16[8,128,1024]{2,1,0:T(8,128)(2,1)}), bf16[1,128,1024]{2,1,0:T(8,128)(2,1)}) %reduce-scatter.10.cloned.1.call-update) | async-done | bytes 262160 | tf_op jit(solution)/shard_map/reduce_scatter | solution.py:68
  406.8 71.4 %reduce-scatter.14.cloned.1.call-done = bf16[1,128,1024]{2,1,0:T(8,128)(2,1)} async-done(((bf16[8,128,1024]{2,1,0:T(8,128)(2,1)}), bf16[1,128,1024]{2,1,0:T(8,128)(2,1)}) %reduce-scatter.14.cloned.1.call-update) | async-done | bytes 262160 | tf_op jit(solution)/shard_map/reduce_scatter | solution.py:68
  (68 shorter events, 1.0 us)
Async XLA Ops:
  7.2 55.1 %all-gather.16.cloned.1.call-start = ((), (), s32[]{:S(2)}) async-start(), calls=%async_computation.14 | async-start | bytes 2359296 | tf_op jit(solution)/shard_map/all_gather | solution.py:32
  7.9 104.2 %all-gather.18.cloned.1.call-start = ((), (), s32[]{:S(2)}) async-start(), calls=%async_computation.15 | async-start | bytes 2359296 | tf_op jit(solution)/shard_map/all_gather | solution.py:33
  8.6 143.0 %reduce-scatter.8.cloned.1.call-start = ((), (), s32[]{:S(2)}) async-start(), calls=%async_computation.7 | async-start | bytes 3932160 | tf_op jit(solution)/shard_map/reduce_scatter | solution.py:53
  62.3 2.3 copy-start.1
  62.3 3.8 copy-start.16
  64.6 57.4 %copy-start.7 = (bf16[8,96,1024]{2,1,0:T(8,128)(2,1)}, bf16[8,96,1024]{2,1,0:T(8,128)(2,1)S(1)}, u32[]{:S(2)}) copy-start(bf16[8,96,1024]{2,1,0:T(8,128)(2,1)S(1)} %convolution_convert_fusion.2) | copy-start | bytes 4718596
  65.2 60.5 %copy-start.5 = (bf16[8,96,1024]{2,1,0:T(8,128)(2,1)}, bf16[8,96,1024]{2,1,0:T(8,128)(2,1)S(1)}, u32[]{:S(2)}) copy-start(bf16[8,96,1024]{2,1,0:T(8,128)(2,1)S(1)} %convolution_convert_fusion.3) | copy-start | bytes 4718596
  71.6 120.9 %reduce-scatter.12.cloned.1.call-start = ((), (), s32[]{:S(2)}) async-start(), calls=%async_computation.10 | async-start | bytes 3932160 | tf_op jit(solution)/shard_map/reduce_scatter | solution.py:53
  112.1 2.3 copy-start
  112.1 3.7 copy-start.14
  114.4 3.2 copy-start.11
  115.0 2.7 copy-start.9
  121.5 111.9 %reduce-scatter.6.cloned.1.call-start = ((), (), s32[]{:S(2)}) async-start(), calls=%async_computation.6 | async-start | bytes 3932160 | tf_op jit(solution)/shard_map/reduce_scatter | solution.py:53
  122.0 3.7 copy-start.18
  129.5 143.5 %all-gather.10.cloned.1.call-start = ((), (), s32[]{:S(2)}) async-start(), calls=%async_computation.8 | async-start | bytes 3932160 | tf_op jit(solution)/shard_map/all_gather | solution.py:58
  151.6 90.1 %copy-start.2 = (bf16[384,1024]{1,0:T(8,128)(2,1)S(1)}, bf16[384,1024]{1,0:T(8,128)(2,1)}, u32[]{:S(2)}) copy-start(bf16[384,1024]{1,0:T(8,128)(2,1)} %reduce-scatter.8.cloned.1.call-done) | copy-start | bytes 2359300
  192.5 49.2 %copy-start.3 = (bf16[384,1024]{1,0:T(8,128)(2,1)S(1)}, bf16[384,1024]{1,0:T(8,128)(2,1)}, u32[]{:S(2)}) copy-start(bf16[384,1024]{1,0:T(8,128)(2,1)} %reduce-scatter.12.cloned.1.call-done) | copy-start | bytes 2359300
  233.4 8.3 %copy-start.4 = (bf16[384,1024]{1,0:T(8,128)(2,1)S(1)}, bf16[384,1024]{1,0:T(8,128)(2,1)}, u32[]{:S(2)}) copy-start(bf16[384,1024]{1,0:T(8,128)(2,1)} %reduce-scatter.6.cloned.1.call-done) | copy-start | bytes 2359300
  244.3 59.3 %all-gather.14.cloned.1.call-start = ((), (), s32[]{:S(2)}) async-start(), calls=%async_computation.12 | async-start | bytes 3932160 | tf_op jit(solution)/shard_map/all_gather | solution.py:58
  245.1 89.2 %all-gather.12.cloned.1.call-start = ((), (), s32[]{:S(2)}) async-start(), calls=%async_computation.11 | async-start | bytes 3932160 | tf_op jit(solution)/shard_map/all_gather | solution.py:58
  245.8 161.0 %reduce-scatter.10.cloned.1.call-start = ((), (), s32[]{:S(2)}) async-start(), calls=%async_computation.9 | async-start | bytes 2359296 | tf_op jit(solution)/shard_map/reduce_scatter | solution.py:68
  273.0 4.8 copy-start.20
  277.0 2.2 copy-start.15
  283.1 195.1 %reduce-scatter.14.cloned.1.call-start = ((), (), s32[]{:S(2)}) async-start(), calls=%async_computation.13 | async-start | bytes 2359296 | tf_op jit(solution)/shard_map/reduce_scatter | solution.py:68
  334.3 4.9 copy-start.22
  338.4 2.2 copy-start.17
  340.6 2.2 copy-start.19
  340.6 3.2 copy-start.24
  347.8 12.2 %copy-start.13 = (s32[128,8]{0,1:T(8,128)S(1)}, s32[128,8]{0,1:T(8,128)}, u32[]{:S(2)}) copy-start(s32[128,8]{0,1:T(8,128)} %param.8) | copy-start | bytes 12292
  347.8 12.8 %copy-start.8 = (bf16[8,96,1024]{2,1,0:T(8,128)(2,1)S(1)}, bf16[8,96,1024]{2,1,0:T(8,128)(2,1)}, u32[]{:S(2)}) copy-start(bf16[8,96,1024]{2,1,0:T(8,128)(2,1)} %copy-done.7) | copy-start | bytes 4718596
  360.7 3.4 copy-start.6
  360.7 3.4 copy-start.25
  366.0 3.4 copy-start.23
  373.1 2.5 copy-start.12
  373.1 3.9 copy-start.21
  377.0 1.9 copy-start.10
Sparse Core Ops, SparseCore 0:
  10.1 52.1 all-gather.15
  64.4 47.6 all-gather.17
  115.2 36.4 reduce-scatter.7
  154.6 37.8 reduce-scatter.11
  195.5 37.8 reduce-scatter.5
  244.5 28.4 all-gather.9
  275.1 28.4 all-gather.13
  305.8 28.4 all-gather.11
  338.4 68.3 reduce-scatter.9
  410.8 67.3 reduce-scatter.13
where the time goes:
time: 492 us; the launch traced here: 485 us
  waiting for transfers between devices  336 us (68%)
  matrix products  54.6 us (11%)
  blocking collectives  49.9 us (10%)
  other arithmetic  20.2 us (4%)
  between operations  14.8 us (3%)
  local copies, waits for them, and re-layouts  8.33 us (2%)
    reduce_scatter x3, waiting for transfers between devices, scatter_rows(): lax.psum_scatter(jnp.concatenate(parts, axis=0), 'tensor', scatter_dimens...  104 us
    reduce_scatter x2, waiting for transfers between devices, combine(): lax.psum_scatter(total_sum.astype(BF16), 'expert', scatter_dimension=0, t...  95.1 us
    all_gather x3, waiting for transfers between devices, gather_rows(): full = lax.all_gather(value.astype(BF16), 'tensor', axis=0, tiled=True)  74.2 us
    dot_general x27, matrix products, dot(): return jnp.einsum(form, left, right, preferred_element_type=F32)  54.6 us
    all_gather x1, waiting for transfers between devices, per_device(): cotangent_all = lax.all_gather(out_cotangent, 'expert', axis=0)  40.4 us
    all_gather x1, blocking collectives, per_device(): weights_all = lax.all_gather(dense_weight, 'expert', axis=0)  32.6 us
    all_gather x1, waiting for transfers between devices, per_device(): tokens_all = lax.all_gather(tokens, 'expert', axis=0)  20 us
    all_to_all x1, blocking collectives, per_device(): lax.all_to_all(pair_tok.transpose(1, 0, 2), 'expert', split_axis=0, conca...  12.2 us
  transfers between devices with their start and end apart: 10, of which 10 were waited for; matrix products, arithmetic and copies ran while one was open for 14% of the time, Pallas kernels for 0%

commit v1 on v0

--- a/solution.py
+++ b/solution.py
@@ -55,7 +55,15 @@
         ).astype(F32)
 
     def gather_rows(value):
-        full = lax.all_gather(value.astype(BF16), "tensor", axis=0, tiled=True)
+        shard = value.astype(BF16)
+        ways, here = (lax.axis_size("tensor"), lax.axis_index("tensor"))
+        full, reach = (shard, 1)
+        while reach < ways:
+            theirs = lax.ppermute(full, "tensor", [(d, d ^ reach) for d in range(ways)])
+            mine_first = jnp.concatenate([full, theirs], axis=0)
+            theirs_first = jnp.concatenate([theirs, full], axis=0)
+            full = jnp.where(here & reach == 0, mine_first, theirs_first)
+            reach = 2 * reach
         return full.reshape(local, slots, hidden)
 
     def combine(parts):

time: 492 us -> 450 us (0.915)
  waiting for transfers between devices: 336 us -> 282 us
  other arithmetic: 20.2 us -> 37.5 us
  matrix products: 54.6 us -> 48 us
    ppermute x0 -> x6, waiting for transfers between devices: none -> 83.7 us  [gather_rows(): theirs = lax.ppermute(full, 'tensor', [(d, d ^ reach) for d in range(ways)])]
    all_gather x3 -> x0, waiting for transfers between devices: 74.2 us -> none  [gather_rows(): full = lax.all_gather(value.astype(BF16), 'tensor', axis=0, tiled=True)]
    reduce_scatter x2, waiting for transfers between devices: 95.1 us -> 32.7 us  [combine(): lax.psum_scatter(total_sum.astype(BF16), 'expert', scatter_dimension=0, t...]
    select_n x0 -> x6, other arithmetic: none -> 17.5 us  [gather_rows(): full = jnp.where(here & reach == 0, mine_first, theirs_first)]
    dot_general x27, matrix products: 54.6 us -> 48 us  [dot(): return jnp.einsum(form, left, right, preferred_element_type=F32)]
  transfers between devices with their start and end apart: 10 -> 13, of which waited for: 10 -> 11; matrix products, arithmetic and copies ran while one was open for 14% -> 18% of each run, Pallas kernels for 0% -> 0%
where the time goes in v1:
time: 450 us; the launch traced here: 442 us
  waiting for transfers between devices  282 us (63%)
  blocking collectives  50 us (11%)
  matrix products  48 us (11%)
  other arithmetic  37.5 us (8%)
  between operations  14.8 us (3%)
  local copies, waits for them, and re-layouts  5.67 us (1%)
    reduce_scatter x3, waiting for transfers between devices, scatter_rows(): lax.psum_scatter(jnp.concatenate(parts, axis=0), 'tensor', scatter_dimens...  104 us
    ppermute x6, waiting for transfers between devices, gather_rows(): theirs = lax.ppermute(full, 'tensor', [(d, d ^ reach) for d in range(ways)])  83.7 us
    dot_general x27, matrix products, dot(): return jnp.einsum(form, left, right, preferred_element_type=F32)  48 us
    all_gather x1, waiting for transfers between devices, per_device(): cotangent_all = lax.all_gather(out_cotangent, 'expert', axis=0)  40.4 us
    reduce_scatter x2, waiting for transfers between devices, combine(): lax.psum_scatter(total_sum.astype(BF16), 'expert', scatter_dimension=0, t...  32.7 us
    all_gather x1, blocking collectives, per_device(): weights_all = lax.all_gather(dense_weight, 'expert', axis=0)  32.6 us
    all_gather x1, waiting for transfers between devices, per_device(): tokens_all = lax.all_gather(tokens, 'expert', axis=0)  20 us
    select_n x6, other arithmetic, gather_rows(): full = jnp.where(here & reach == 0, mine_first, theirs_first)  17.5 us
  transfers between devices with their start and end apart: 13, of which 11 were waited for; matrix products, arithmetic and copies ran while one was open for 18% of the time, Pallas kernels for 0%

profile of v1, /device:TPU:0, one launch (start us, length us, event | category | flops | bytes accessed | tf_op | source)
XLA Modules:
  0.0 442.4 jit_solution(11744010813135485296)
XLA Ops:
  7.2 0.7 all-gather.7.cloned.1.call-update
  7.9 0.7 all-gather.9.cloned.1.call-update
  8.7 0.7 select_reduce_fusion.3
  9.4 32.6 %all-gather = f32[1024,16]{0,1:T(8,128)S(1)} all-gather(f32[128,16]{0,1:T(8,128)S(1)} %select_reduce_fusion.3), channel_id=2, replica_groups=mesh['expert'=8,'tensor'=4] {'expert'}, dimensions={0}, use_global_device_ids=true | all-gather | bytes 73728 | tf_op jit(solution)/shard_map/all_gather | solution.py:31
  42.3 20.0 %all-gather.7.cloned.1.call-done = bf16[1024,1024]{1,0:T(8,128)(2,1)} async-done(((bf16[128,1024]{1,0:T(8,128)(2,1)}), bf16[1024,1024]{1,0:T(8,128)(2,1)}) %all-gather.7.cloned.1.call-update) | async-done | bytes 2097168 | tf_op jit(solution)/shard_map/all_gather | solution.py:32
  62.3 2.3 convolution_convert_fusion.2
  65.2 0.8 copy-done.22
  66.0 1.8 fusion.46
  67.8 1.8 fusion.43
  69.7 2.0 pad_maximum_fusion.4
  71.7 40.4 %all-gather.9.cloned.1.call-done = bf16[1024,1024]{1,0:T(8,128)(2,1)} async-done(((bf16[128,1024]{1,0:T(8,128)(2,1)}), bf16[1024,1024]{1,0:T(8,128)(2,1)}) %all-gather.9.cloned.1.call-update) | async-done | bytes 2097168 | tf_op jit(solution)/shard_map/all_gather | solution.py:33
  112.1 2.3 convolution_convert_fusion
  115.0 0.8 copy-done.20
  115.8 1.8 fusion.58
  117.7 1.8 fusion.52
  119.5 2.0 pad_maximum_fusion.5
  122.1 3.6 fusion.40
  125.7 1.8 fusion.37
  127.5 2.0 pad_maximum_fusion.3
  129.6 22.1 %reduce-scatter.8.cloned.1.call-done = bf16[384,1024]{1,0:T(8,128)(2,1)} async-done(((bf16[1536,1024]{1,0:T(8,128)(2,1)}), bf16[384,1024]{1,0:T(8,128)(2,1)}) %reduce-scatter.8.cloned.1.call-update) | async-done | bytes 786448 | tf_op jit(solution)/shard_map/reduce_scatter | solution.py:53
  151.7 40.9 %reduce-scatter.12.cloned.1.call-done = bf16[384,1024]{1,0:T(8,128)(2,1)} async-done(((bf16[1536,1024]{1,0:T(8,128)(2,1)}), bf16[384,1024]{1,0:T(8,128)(2,1)}) %reduce-scatter.12.cloned.1.call-update) | async-done | bytes 786448 | tf_op jit(solution)/shard_map/reduce_scatter | solution.py:53
  192.5 40.9 %reduce-scatter.6.cloned.1.call-done = bf16[384,1024]{1,0:T(8,128)(2,1)} async-done(((bf16[1536,1024]{1,0:T(8,128)(2,1)}), bf16[384,1024]{1,0:T(8,128)(2,1)}) %reduce-scatter.6.cloned.1.call-update) | async-done | bytes 786448 | tf_op jit(solution)/shard_map/reduce_scatter | solution.py:53
  233.4 2.3 fusion.65
  235.7 5.2 %all-gather.3 = f32[4,1,384]{2,1,0:T(1,128)S(1)} all-gather(f32[1,1,384]{2,1,0:T(1,128)S(1)} %reshape.84), channel_id=1, replica_groups=mesh['expert'=8,'tensor'=4] {'tensor'}, dimensions={0}, use_global_device_ids=true | all-gather | bytes 7680 | tf_op jit(solution)/shard_map/all_gather | solution.py:99
  241.0 0.6 select_reduce_fusion
  241.8 2.3 fusion.64
  245.0 1.4 collective-permute-done
  246.4 2.1 maximum_select_fusion.3
  249.4 1.9 collective-permute-done.4
  251.3 2.7 maximum_select_fusion.5
  254.0 1.8 collective-permute-start.5
  255.7 3.8 maximum_select_fusion.4
  259.9 26.0 %collective-permute-done.1 = bf16[768,1024]{1,0:T(8,128)(2,1)} collective-permute-done((bf16[768,1024]{1,0:T(8,128)(2,1)S(1)}, bf16[768,1024]{1,0:T(8,128)(2,1)}, u32[]{:S(2)}, u32[]{:S(2)}) %collective-permute-start.1) | collective-permute-done | bytes 1572896 | tf_op jit(solution)/shard_map/ppermute | solution.py:62
  285.9 2.8 maximum_select_fusion
  288.7 1.8 fusion.49
  290.5 1.8 fusion.55
  292.3 0.8 fusion.88
  293.1 2.1 add_convert_fusion.1
  295.5 24.1 %collective-permute-done.5 = bf16[768,1024]{1,0:T(8,128)(2,1)} collective-permute-done((bf16[768,1024]{1,0:T(8,128)(2,1)S(1)}, bf16[768,1024]{1,0:T(8,128)(2,1)}, u32[]{:S(2)}, u32[]{:S(2)}) %collective-permute-start.5) | collective-permute-done | bytes 1572896 | tf_op jit(solution)/shard_map/ppermute | solution.py:62
  319.6 2.8 maximum_select_fusion.2
  322.4 30.3 %collective-permute-done.3 = bf16[768,1024]{1,0:T(8,128)(2,1)} collective-permute-done((bf16[768,1024]{1,0:T(8,128)(2,1)}, bf16[768,1024]{1,0:T(8,128)(2,1)}, u32[]{:S(2)}, u32[]{:S(2)}) %collective-permute-start.3) | collective-permute-done | bytes 1572896 | tf_op jit(solution)/shard_map/ppermute | solution.py:62
  352.7 3.3 maximum_select_fusion.1
  356.1 1.8 fusion.12
  358.3 1.8 add_convert_fusion.3
  360.1 0.8 fusion.87
  360.9 1.8 fusion.8
  362.7 1.8 add_convert_fusion.2
  364.5 2.2 add_convert_fusion
  366.8 12.2 %all_to_all.5 = f32[8,2,128]{2,1,0:T(2,128)S(1)} all-to-all(f32[8,2,128]{2,1,0:T(2,128)S(1)} %copy.26), channel_id=1, replica_groups=mesh['expert'=8,'tensor'=4] {'expert'}, dimensions={0} | all-to-all | bytes 16384 | tf_op jit(solution)/shard_map/all_to_all | solution.py:102
  379.0 0.6 select_reduce_fusion.2
  379.6 3.4 convert_bitcast_fusion.4
  383.0 1.9 convert_bitcast_fusion.5
  384.9 2.5 pad_maximum_fusion
  387.4 0.8 copy-done.5
  388.2 0.6 copy-done.14
  388.8 1.9 convert_bitcast_fusion.2
  390.7 1.9 convert_bitcast_fusion.3
  392.6 2.5 pad_maximum_fusion.1
  395.1 0.8 copy-done.3
  395.9 0.6 copy-done.18
  396.5 1.9 convert_bitcast_fusion
  398.3 1.9 convert_bitcast_fusion.1
  400.2 2.4 pad_maximum_fusion.2
  402.6 32.7 %reduce-scatter.14.cloned.1.call-done = bf16[1,128,1024]{2,1,0:T(8,128)(2,1)} async-done(((bf16[8,128,1024]{2,1,0:T(8,128)(2,1)}), bf16[1,128,1024]{2,1,0:T(8,128)(2,1)}) %reduce-scatter.14.cloned.1.call-update) | async-done | bytes 262160 | tf_op jit(solution)/shard_map/reduce_scatter | solution.py:76
  (77 shorter events, 5.2 us)
Async XLA Ops:
  7.2 55.1 %all-gather.7.cloned.1.call-start = ((), (), s32[]{:S(2)}) async-start(), calls=%async_computation.11 | async-start | bytes 2359296 | tf_op jit(solution)/shard_map/all_gather | solution.py:32
  7.9 104.2 %all-gather.9.cloned.1.call-start = ((), (), s32[]{:S(2)}) async-start(), calls=%async_computation.12 | async-start | bytes 2359296 | tf_op jit(solution)/shard_map/all_gather | solution.py:33
  8.6 143.0 %reduce-scatter.8.cloned.1.call-start = ((), (), s32[]{:S(2)}) async-start(), calls=%async_computation.7 | async-start | bytes 3932160 | tf_op jit(solution)/shard_map/reduce_scatter | solution.py:53
  62.3 2.3 copy-start.1
  62.3 3.8 copy-start.22
  64.6 57.4 %copy-start.13 = (bf16[8,96,1024]{2,1,0:T(8,128)(2,1)}, bf16[8,96,1024]{2,1,0:T(8,128)(2,1)S(1)}, u32[]{:S(2)}) copy-start(bf16[8,96,1024]{2,1,0:T(8,128)(2,1)S(1)} %convolution_convert_fusion.2) | copy-start | bytes 4718596
  65.2 60.5 %copy-start.11 = (bf16[8,96,1024]{2,1,0:T(8,128)(2,1)}, bf16[8,96,1024]{2,1,0:T(8,128)(2,1)S(1)}, u32[]{:S(2)}) copy-start(bf16[8,96,1024]{2,1,0:T(8,128)(2,1)S(1)} %convolution_convert_fusion.3) | copy-start | bytes 4718596
  71.6 120.9 %reduce-scatter.12.cloned.1.call-start = ((), (), s32[]{:S(2)}) async-start(), calls=%async_computation.9 | async-start | bytes 3932160 | tf_op jit(solution)/shard_map/reduce_scatter | solution.py:53
  112.1 2.3 copy-start
  112.1 3.8 copy-start.20
  114.4 3.3 copy-start.17
  115.0 2.7 copy-start.15
  121.5 111.9 %reduce-scatter.6.cloned.1.call-start = ((), (), s32[]{:S(2)}) async-start(), calls=%async_computation.6 | async-start | bytes 3932160 | tf_op jit(solution)/shard_map/reduce_scatter | solution.py:53
  122.0 3.7 copy-start.24
  129.5 273.0 %reduce-scatter.10.cloned.1.call-start = ((), (), s32[]{:S(2)}) async-start(), calls=%async_computation.8 | async-start | bytes 2359296 | tf_op jit(solution)/shard_map/reduce_scatter | solution.py:76
  151.7 90.1 %copy-start.6 = (bf16[384,1024]{1,0:T(8,128)(2,1)S(1)}, bf16[384,1024]{1,0:T(8,128)(2,1)}, u32[]{:S(2)}) copy-start(bf16[384,1024]{1,0:T(8,128)(2,1)} %reduce-scatter.8.cloned.1.call-done) | copy-start | bytes 2359300
  192.5 49.2 %copy-start.7 = (bf16[384,1024]{1,0:T(8,128)(2,1)S(1)}, bf16[384,1024]{1,0:T(8,128)(2,1)}, u32[]{:S(2)}) copy-start(bf16[384,1024]{1,0:T(8,128)(2,1)} %reduce-scatter.12.cloned.1.call-done) | copy-start | bytes 2359300
  233.4 8.3 %copy-start.8 = (bf16[384,1024]{1,0:T(8,128)(2,1)S(1)}, bf16[384,1024]{1,0:T(8,128)(2,1)}, u32[]{:S(2)}) copy-start(bf16[384,1024]{1,0:T(8,128)(2,1)} %reduce-scatter.6.cloned.1.call-done) | copy-start | bytes 2359300
  244.1 0.9 copy-start.10
  244.1 4.8 %copy-start.9 = (bf16[384,1024]{1,0:T(8,128)(2,1)S(1)}, bf16[384,1024]{1,0:T(8,128)(2,1)}, u32[]{:S(2)}) copy-start(bf16[384,1024]{1,0:T(8,128)(2,1)} %get-tuple-element.9) | copy-start | bytes 2359300
  244.1 2.3 collective-permute-start
  248.5 37.4 %collective-permute-start.1 = (bf16[768,1024]{1,0:T(8,128)(2,1)S(1)}, bf16[768,1024]{1,0:T(8,128)(2,1)}, u32[]{:S(2)}, u32[]{:S(2)}) collective-permute-start(bf16[768,1024]{1,0:T(8,128)(2,1)S(1)} %maximum_select_fusion.3), channel_id=1, source_target_pairs={{0,2},{1,3},{2,0},{3,1},{4,6},{5,7},{6,4},{7,5},{8,10},{9,11},{10,... | collective-permute-start | bytes 4718600 | tf_op jit(solution)/shard_map/ppermute | solution.py:62
  248.9 2.4 collective-permute-start.4
  249.0 6.8 %collective-permute-start.2 = (bf16[384,1024]{1,0:T(8,128)(2,1)}, bf16[384,1024]{1,0:T(8,128)(2,1)}, u32[]{:S(2)}, u32[]{:S(2)}) collective-permute-start(bf16[384,1024]{1,0:T(8,128)(2,1)} %get-tuple-element.8), channel_id=1, source_target_pairs={{0,1},{1,0},{2,3},{3,2},{4,5},{5,4},{6,7},{7,6},{8,9},{9,8},{10,11... | collective-permute-start | bytes 2359304 | tf_op jit(solution)/shard_map/ppermute | solution.py:62
  254.0 65.7 %collective-permute-start.5 = (bf16[768,1024]{1,0:T(8,128)(2,1)S(1)}, bf16[768,1024]{1,0:T(8,128)(2,1)}, u32[]{:S(2)}, u32[]{:S(2)}) collective-permute-start(bf16[768,1024]{1,0:T(8,128)(2,1)S(1)} %maximum_select_fusion.5), channel_id=1, source_target_pairs={{0,2},{1,3},{2,0},{3,1},{4,6},{5,7},{6,4},{7,5},{8,10},{9,11},{10,... | collective-permute-start | bytes 4718600 | tf_op jit(solution)/shard_map/ppermute | solution.py:62
  259.6 29.1 %copy-start.21 = (bf16[2,1024,1024]{2,1,0:T(8,128)(2,1)S(1)}, bf16[2,1024,1024]{2,1,0:T(8,128)(2,1)}, u32[]{:S(2)}) copy-start(bf16[2,1024,1024]{2,1,0:T(8,128)(2,1)} %param.12) | copy-start | bytes 12582916
  259.6 93.1 %collective-permute-start.3 = (bf16[768,1024]{1,0:T(8,128)(2,1)}, bf16[768,1024]{1,0:T(8,128)(2,1)}, u32[]{:S(2)}, u32[]{:S(2)}) collective-permute-start(bf16[768,1024]{1,0:T(8,128)(2,1)} %maximum_select_fusion.4), channel_id=1, source_target_pairs={{0,2},{1,3},{2,0},{3,1},{4,6},{5,7},{6,4},{7,5},{8,10},{9,11},{10,... | collective-permute-start | bytes 4718600 | tf_op jit(solution)/shard_map/ppermute | solution.py:62
  288.7 1.8 copy-start.2
  295.3 140.0 %reduce-scatter.14.cloned.1.call-start = ((), (), s32[]{:S(2)}) async-start(), calls=%async_computation.10 | async-start | bytes 2359296 | tf_op jit(solution)/shard_map/reduce_scatter | solution.py:76
  322.4 38.5 %copy-start.4 = (bf16[1536,1024]{1,0:T(8,128)(2,1)}, bf16[1536,1024]{1,0:T(8,128)(2,1)S(1)}, u32[]{:S(2)}) copy-start(bf16[1536,1024]{1,0:T(8,128)(2,1)S(1)} %maximum_select_fusion.2) | copy-start | bytes 9437188
  322.4 33.6 %copy-start.23 = (bf16[2,1024,1024]{2,1,0:T(8,128)(2,1)S(1)}, bf16[2,1024,1024]{2,1,0:T(8,128)(2,1)}, u32[]{:S(2)}) copy-start(bf16[2,1024,1024]{2,1,0:T(8,128)(2,1)} %param.11) | copy-start | bytes 12582916
  356.1 2.2 copy-start.25
  366.7 12.3 %copy-start.19 = (s32[128,8]{0,1:T(8,128)S(1)}, s32[128,8]{0,1:T(8,128)}, u32[]{:S(2)}) copy-start(s32[128,8]{0,1:T(8,128)} %param.8) | copy-start | bytes 12292
  379.6 3.4 copy-start.12
  384.9 3.3 copy-start.5
  384.9 3.9 copy-start.14
  392.5 3.3 copy-start.3
  392.6 3.9 copy-start.18
  396.4 1.9 copy-start.16
Sparse Core Ops, SparseCore 0:
  10.1 52.1 all-gather.6
  64.4 47.6 all-gather.8
  115.2 36.4 reduce-scatter.7
  154.6 37.8 reduce-scatter.11
  195.5 37.8 reduce-scatter.5
  295.4 68.2 reduce-scatter.9
  367.8 67.4 reduce-scatter.13
